TPU v7x, 32 devices: a whole 2x2x4 slice. The times are simulated.
32 devices in a mesh: grp: 4 (over y, x), sub: 8 (over z, core).
Axes of the slice: x: 2, y: 2, z: 4, core: 2. Of those that a mesh axis runs over, the one named last changes fastest.
Arguments:
- right_side: float32 [24576, 160], P(('grp', 'sub')), may hold values from -6 to 6
- iterate_in: float32 [24576, 160], P(('grp', 'sub')), may hold values from -6 to 6
- diagonal: float32 [24576], P(('grp', 'sub')), may hold values from 1.5 to 4
- block_values: bfloat16 [32, 6, 3, 128, 128], P(('grp', 'sub')), may hold values from -0.125 to 0.125
- block_cols: int32 [32, 6, 3], P(('grp', 'sub')), may hold values from 0 to 5, as said below
- couple_left: bfloat16 [24576, 128], P(('grp', 'sub')), may hold values from -0.125 to 0.125
- couple_right: bfloat16 [24576, 128], P(('grp', 'sub')), may hold values from -0.125 to 0.125
- send_rows: int32 [32, 2, 128], P(('grp', 'sub')), may hold values from 0 to 767, as said below
- local_inverse: bfloat16 [32, 1024, 1024], P(('grp', 'sub')), may hold values from -0.3 to 2.3, as said below
- coarse_basis: bfloat16 [32, 1024, 32], P(('grp', 'sub')), may hold values from -0.1875 to 0.1875
- coarse_diag: float32 [32, 32, 32], P(('grp', 'sub')), may hold values from -54 to 59.5, as said below
- coarse_up: float32 [32, 32, 32], P(('grp', 'sub')), may hold values from -29.7 to 27
Outputs:
- iterate: float32 [24576, 160], P(('grp', 'sub'))
- residual: float32 [24576, 160], P(('grp', 'sub'))
Inputs may be any that keep to these rules, and one draw needn't show every extreme that they name: `block_cols`: the 3 column blocks of one row block are distinct. `send_rows`: the 256 rows listed for one subdomain are distinct. `local_inverse`: each block is symmetric positive definite. `coarse_diag`: each block is symmetric; with coarse_up the coarse operator is symmetric positive definite.
All inputs are finite; a program needn't handle non-finite values.
Results may differ from a plain program's by a relative error of at most 0.0032.
Values may be sent and summed in bfloat16 or wider, within the bound.
No kernel may reach another device: no remote copies, remote signals or barrier semaphores. Data moves between devices by JAX's collectives and lax.ppermute only.
A program may use at most 64 MiB of HBM per device.

v0:
```python
import jax
import jax.numpy as jnp
from jax import lax
from jax.sharding import PartitionSpec as P


def with_halo(cells, sides, width):
    for axis, dim in sides:
        count = lax.axis_size(axis)
        ends = count - 1
        head = lax.slice_in_dim(cells, 0, width, axis=dim)
        tail = lax.slice_in_dim(cells, cells.shape[dim] - width, cells.shape[dim], axis=dim)
        cells = jnp.concatenate(
            [
                lax.ppermute(tail, axis, [(i, (i + 1) % count) for i in range(ends)]),
                cells,
                lax.ppermute(head, axis, [((i + 1) % count, i) for i in range(ends)]),
            ],
            axis=dim,
        )
    return cells


def chol_solve(factor, values):
    halfway = lax.linalg.triangular_solve(factor, values, left_side=True, lower=True)
    return lax.linalg.triangular_solve(
        factor, halfway, left_side=True, lower=True, transpose_a=True
    )


def solve_chain(diagonal_blocks, upper, values):
    highest = lax.Precision.HIGHEST
    blocks_total = diagonal_blocks.shape[0]
    padded_total = 1
    while padded_total < blocks_total:
        padded_total = padded_total * 2
    extra = padded_total - blocks_total
    block_width = diagonal_blocks.shape[1]
    identity = jnp.eye(block_width, dtype=jnp.float32)
    diag_now = jnp.concatenate(
        [diagonal_blocks, jnp.broadcast_to(identity, (extra, block_width, block_width))], axis=0
    )
    upper_now = jnp.concatenate(
        [upper[:-1], jnp.zeros((extra + 1, block_width, block_width), jnp.float32)], axis=0
    )
    rhs_now = jnp.concatenate([values, jnp.zeros((extra,) + values.shape[1:], jnp.float32)], axis=0)
    levels = []
    while diag_now.shape[0] > 1:
        diag_even = diag_now[0::2]
        diag_odd = diag_now[1::2]
        upper_even = upper_now[0::2]
        upper_odd = upper_now[1::2]
        rhs_even = rhs_now[0::2]
        rhs_odd = rhs_now[1::2]
        factor = jnp.linalg.cholesky(diag_odd)
        stacked = jnp.concatenate([jnp.swapaxes(upper_even, 1, 2), upper_odd, rhs_odd], axis=2)
        through = chol_solve(factor, stacked)
        toward_left = through[:, :, :block_width]
        toward_right = through[:, :, block_width : 2 * block_width]
        odd_loads = through[:, :, 2 * block_width :]
        new_diag = diag_even - jnp.einsum(
            "mab,mbc->mac", upper_even, toward_left, precision=highest
        )
        new_upper = -jnp.einsum("mab,mbc->mac", upper_even, toward_right, precision=highest)
        new_rhs = rhs_even - jnp.einsum("mab,mbn->man", upper_even, odd_loads, precision=highest)
        from_diag = jnp.einsum("mba,mbc->mac", upper_odd, toward_right, precision=highest)
        from_rhs = jnp.einsum("mba,mbn->man", upper_odd, odd_loads, precision=highest)
        new_diag = new_diag - jnp.concatenate(
            [jnp.zeros_like(from_diag[:1]), from_diag[:-1]], axis=0
        )
        new_rhs = new_rhs - jnp.concatenate([jnp.zeros_like(from_rhs[:1]), from_rhs[:-1]], axis=0)
        levels.append((toward_left, toward_right, odd_loads))
        diag_now, upper_now, rhs_now = (new_diag, new_upper, new_rhs)
    solution = chol_solve(jnp.linalg.cholesky(diag_now[0]), rhs_now[0])[None]
    for toward_left, toward_right, odd_loads in reversed(levels):
        next_sol = jnp.concatenate([solution[1:], jnp.zeros_like(solution[:1])], axis=0)
        odd_part = (
            odd_loads
            - jnp.einsum("mab,mbn->man", toward_left, solution, precision=highest)
            - jnp.einsum("mab,mbn->man", toward_right, next_sol, precision=highest)
        )
        solution = jnp.stack([solution, odd_part], axis=1).reshape((-1,) + solution.shape[1:])
    return solution[:blocks_total]


def shards(
    right_side,
    iterate_in,
    diagonal,
    block_values,
    block_cols,
    couple_left,
    couple_right,
    send_rows,
    local_inverse,
    coarse_basis,
    coarse_diag,
    coarse_up,
):
    bf16 = jnp.bfloat16
    f32 = jnp.float32
    highest = lax.Precision.HIGHEST
    intersection = send_rows.shape[2]
    rows_own = right_side.shape[0]
    cases = right_side.shape[1]
    row_blocks = block_cols.shape[1]
    modes = coarse_basis.shape[2]
    column_blocks = block_cols[0]
    sent_left_rows = send_rows[0, 0]
    sent_right_rows = send_rows[0, 1]

    def neighbour_rows(source):
        boundary = jnp.stack([source[sent_left_rows], source[sent_right_rows]])
        padded = with_halo(boundary, ((("grp", "sub"), 0),), 1)
        return (padded[0], padded[3])

    def apply_operator(vector):
        rounded = vector.astype(bf16)
        from_left, from_right = neighbour_rows(rounded)
        blocks = rounded.reshape(row_blocks, -1, cases)
        picked = blocks[column_blocks]
        sparse = jnp.einsum(
            "itab,itbn->ian", block_values[0], picked, preferred_element_type=f32
        ).reshape(rows_own, cases)
        coupled = jnp.dot(couple_left, from_left, preferred_element_type=f32) + jnp.dot(
            couple_right, from_right, preferred_element_type=f32
        )
        return diagonal[:, None] * vector + (sparse + coupled)

    residual_start = right_side - apply_operator(iterate_in)
    rounded = residual_start.astype(bf16)
    from_left, from_right = neighbour_rows(rounded)
    extended = jnp.concatenate([from_left, rounded, from_right], axis=0)
    local_part = jnp.dot(local_inverse[0], extended, preferred_element_type=f32)
    coarse_in = jnp.dot(coarse_basis[0].T, extended, preferred_element_type=f32)
    blocks_diag = lax.all_gather(coarse_diag, "sub", axis=0, tiled=True)
    blocks_up = lax.all_gather(coarse_up, "sub", axis=0, tiled=True)
    group = lax.axis_index("grp")
    groups = lax.axis_size("grp")
    member = lax.axis_index("sub")
    members = lax.axis_size("sub")
    keep = (group < groups - 1).astype(f32)
    first_up = blocks_up[0]
    last_up = blocks_up[members - 1] * keep
    columns = lax.all_gather(coarse_in[None], "sub", axis=0, tiled=True)
    width = columns.shape[2]
    inner_count = members - 1
    empty_cols = jnp.zeros((inner_count, modes, modes), f32)
    left_cols = empty_cols.at[0].set(first_up.T)
    right_cols = empty_cols.at[inner_count - 1].set(last_up)
    stacked = jnp.concatenate([columns[1:], left_cols, right_cols], axis=2)
    solved = solve_chain(blocks_diag[1:], blocks_up[1:], stacked)
    sol_loads = solved[:, :, :width]
    sol_left = solved[:, :, width : width + modes]
    sol_right = solved[:, :, width + modes :]
    self_left = jnp.dot(first_up, sol_left[0], precision=highest)
    cross_term = jnp.dot(first_up, sol_right[0], precision=highest)
    rhs_first = jnp.dot(first_up, sol_loads[0], precision=highest)
    self_right = jnp.dot(last_up.T, sol_right[-1], precision=highest)
    rhs_last = jnp.dot(last_up.T, sol_loads[-1], precision=highest)
    sep_diag = lax.all_gather(blocks_diag[0][None], "grp", axis=0, tiled=True)
    sep_rhs = lax.all_gather(columns[0][None], "grp", axis=0, tiled=True)
    all_left = lax.all_gather(self_left[None], "grp", axis=0, tiled=True)
    all_right = lax.all_gather(self_right[None], "grp", axis=0, tiled=True)
    all_cross = lax.all_gather(cross_term[None], "grp", axis=0, tiled=True)
    all_first = lax.all_gather(rhs_first[None], "grp", axis=0, tiled=True)
    all_last = lax.all_gather(rhs_last[None], "grp", axis=0, tiled=True)
    prev_right = jnp.concatenate([jnp.zeros_like(all_right[:1]), all_right[:-1]], axis=0)
    prev_last = jnp.concatenate([jnp.zeros_like(all_last[:1]), all_last[:-1]], axis=0)
    reduced_diag = sep_diag - all_left - prev_right
    reduced_rhs = sep_rhs - all_first - prev_last
    sep_sol = solve_chain(reduced_diag, -all_cross, reduced_rhs)
    padded_sol = jnp.concatenate([sep_sol, jnp.zeros_like(sep_sol[:1])], axis=0)
    mine = lax.dynamic_index_in_dim(padded_sol, group, 0, keepdims=False)
    after = lax.dynamic_index_in_dim(padded_sol, group + 1, 0, keepdims=False)
    inner_sol = (
        sol_loads
        - jnp.einsum("ivw,wn->ivn", sol_left, mine, precision=highest)
        - jnp.einsum("ivw,wn->ivn", sol_right, after, precision=highest)
    )
    group_sol = jnp.concatenate([mine[None], inner_sol], axis=0)
    coarse_sol = lax.dynamic_index_in_dim(group_sol, member, 0, keepdims=False)
    correction = local_part + jnp.dot(
        coarse_basis[0], coarse_sol.astype(bf16), preferred_element_type=f32
    )
    tails = jnp.stack([correction[:intersection], correction[intersection + rows_own :]])
    returned = with_halo(tails.astype(jnp.bfloat16), ((("grp", "sub"), 0),), 1).astype(tails.dtype)
    owned = correction[intersection : intersection + rows_own]
    owned = owned.at[sent_right_rows].add(returned[3])
    owned = owned.at[sent_left_rows].add(returned[0])
    inner = lax.psum(jnp.sum(residual_start * owned, axis=0), ("grp", "sub"))
    image = apply_operator(owned)
    curvature = lax.psum(jnp.sum(owned * image, axis=0), ("grp", "sub"))
    step_size = inner / curvature
    return (iterate_in + step_size * owned, residual_start - step_size * image)


def solution(mesh):
    in_specs = (
        P(("grp", "sub"), None),
        P(("grp", "sub"), None),
        P(("grp", "sub")),
        P(("grp", "sub"), None, None, None, None),
        P(("grp", "sub"), None, None),
        P(("grp", "sub"), None),
        P(("grp", "sub"), None),
        P(("grp", "sub"), None, None),
        P(("grp", "sub"), None, None),
        P(("grp", "sub"), None, None),
        P(("grp", "sub"), None, None),
        P(("grp", "sub"), None, None),
    )
    out_specs = (P(("grp", "sub"), None), P(("grp", "sub"), None))
    return jax.shard_map(shards, mesh=mesh, in_specs=in_specs, out_specs=out_specs, check_vma=False)
```

profile of v0, /device:TPU:14, one launch (start us, length us, event | category | flops | bytes accessed | tf_op | source)
XLA Modules:
  0.0 289.2 jit_solution(11546375033526299166)
XLA Ops:
  7.7 2.4 collective-permute-start
  10.4 14.8 %all_gather.32 = f32[8,32,32]{2,1,0:T(8,128)S(1)} all-gather(f32[1,32,32]{2,1,0:T(8,128)S(1)} %copy-done.34), channel_id=1, replica_groups=mesh['grp'=4,'sub'=8] {'sub'}, dimensions={0}, use_global_device_ids=true | all-gather | bytes 36864 | tf_op jit(solution)/shard_map/all_gather | solution.py:137
  25.2 14.0 %all_gather.30 = f32[8,32,32]{2,1,0:T(8,128)S(1)} all-gather(f32[1,32,32]{2,1,0:T(8,128)S(1)} %copy-done.35), channel_id=1, replica_groups=mesh['grp'=4,'sub'=8] {'sub'}, dimensions={0}, use_global_device_ids=true | all-gather | bytes 36864 | tf_op jit(solution)/shard_map/all_gather | solution.py:136
  39.5 11.7 %custom-call.47 = f32[4,32,32]{2,1,0:T(8,128)S(1)} custom-call(f32[4,32,32]{2,1,0:T(8,128)S(1)} %copy.185), custom_call_target="Cholesky" | custom-call | tf_op jit(solution)/shard_map/jit(cholesky)/cholesky | solution.py:55
  61.8 4.0 %collective-permute-start.3 = (bf16[1,128,160]{1,2,0:T(8,128)(2,1)S(1)}, bf16[1,128,160]{1,2,0:T(8,128)(2,1)S(1)}, u32[]{:S(2)}, u32[]{:S(2)}) collective-permute-start(bf16[1,128,160]{1,2,0:T(8,128)(2,1)S(1)} %bitcast.412), channel_id=1, source_target_pairs={{1,0},{2,1},{3,2},{4,3},{5,4},{6,5},{7,6},{8,7},{9,8},{10,9},{11,1... | collective-permute-start | bytes 122888 | tf_op jit(solution)/shard_map/ppermute | solution.py:17
  68.7 11.2 %custom-call.48 = f32[4,1,32,32]{2,3,1,0:T(8,128)} custom-call(f32[4,1,32,32]{3,2,1,0:T(8,128)} %select_bitcast_fusion), custom_call_target="InvertDiagBlocksLowerTriangular" | custom-call | tf_op jit(solution)/shard_map/triangular_solve | solution.py:26
  79.9 9.1 %all_gather.31 = f32[4,32,32]{2,1,0:T(8,128)S(1)} all-gather(f32[1,32,32]{2,1,0:T(8,128)S(1)} %slice-done.1), channel_id=1, replica_groups=mesh['grp'=4,'sub'=8] {'grp'}, dimensions={0}, use_global_device_ids=true | all-gather | bytes 20480 | tf_op jit(solution)/shard_map/all_gather | solution.py:161
  90.5 12.7 %all-gather = f32[256,160]{1,0:T(8,128)S(1)} all-gather(f32[32,160]{1,0:T(8,128)S(1)} %convolution_bitcast_fusion.11), channel_id=2, replica_groups=mesh['grp'=4,'sub'=8] {'sub'}, dimensions={0}, use_global_device_ids=true | all-gather | bytes 184320 | tf_op jit(solution)/shard_map/all_gather | solution.py:145
  106.0 5.9 %custom-call.57 = f32[2,32,32]{2,1,0:T(8,128)S(1)} custom-call(f32[2,32,32]{2,1,0:T(8,128)S(1)} %fusion.117), custom_call_target="Cholesky" | custom-call | tf_op jit(solution)/shard_map/jit(cholesky)/cholesky | solution.py:55
  112.1 4.9 %custom-call.49 = f32[2,1,32,32]{2,3,1,0:T(8,128)S(1)} custom-call(f32[2,1,32,32]{3,2,1,0:T(8,128)S(1)} %fusion.119), custom_call_target="InvertDiagBlocksLowerTriangular" | custom-call | tf_op jit(solution)/shard_map/triangular_solve | solution.py:26
  119.1 2.9 %custom-call.58 = f32[1,32,32]{2,1,0:T(8,128)S(1)} custom-call(f32[1,32,32]{2,1,0:T(8,128)S(1)} %fusion.169), custom_call_target="Cholesky" | custom-call | tf_op jit(solution)/shard_map/jit(cholesky)/cholesky | solution.py:55
  123.2 2.4 custom-call.50
  126.9 2.9 %cholesky.184 = f32[32,32]{1,0:T(8,128)S(1)} custom-call(f32[32,32]{1,0:T(8,128)S(1)} %fusion.150), custom_call_target="Cholesky" | custom-call | tf_op jit(solution)/shard_map/jit(cholesky)/cholesky | solution.py:74
  131.1 2.4 custom-call.51
  136.5 7.0 %all-gather.6 = f32[128,160]{1,0:T(8,128)S(1)} all-gather(f32[32,160]{1,0:T(8,128)S(1)} %slice-done), channel_id=8, replica_groups=mesh['grp'=4,'sub'=8] {'grp'}, dimensions={0}, use_global_device_ids=true | all-gather | bytes 102400 | tf_op jit(solution)/shard_map/all_gather | solution.py:162
  143.4 8.9 %all-gather.4 = f32[128,160]{1,0:T(8,128)S(1)} all-gather(f32[32,160]{1,0:T(8,128)S(1)} %convolution_bitcast_fusion.7), channel_id=6, replica_groups=mesh['grp'=4,'sub'=8] {'grp'}, dimensions={0}, use_global_device_ids=true | all-gather | bytes 102400 | tf_op jit(solution)/shard_map/all_gather | solution.py:166
  152.4 7.1 %all-gather.5 = f32[128,160]{1,0:T(8,128)S(1)} all-gather(f32[32,160]{1,0:T(8,128)S(1)} %fusion.101), channel_id=7, replica_groups=mesh['grp'=4,'sub'=8] {'grp'}, dimensions={0}, use_global_device_ids=true | all-gather | bytes 102400 | tf_op jit(solution)/shard_map/all_gather | solution.py:167
  159.6 8.7 %all-gather.3 = f32[128,32]{1,0:T(8,128)S(1)} all-gather(f32[32,32]{1,0:T(8,128)S(1)} %copy.214), channel_id=5, replica_groups=mesh['grp'=4,'sub'=8] {'grp'}, dimensions={0}, use_global_device_ids=true | all-gather | bytes 20480 | tf_op jit(solution)/shard_map/all_gather | solution.py:165
  168.5 6.7 %all-gather.2 = f32[128,32]{1,0:T(8,128)S(1)} all-gather(f32[32,32]{1,0:T(8,128)S(1)} %fusion.145), channel_id=4, replica_groups=mesh['grp'=4,'sub'=8] {'grp'}, dimensions={0}, use_global_device_ids=true | all-gather | bytes 20480 | tf_op jit(solution)/shard_map/all_gather | solution.py:164
  175.4 8.9 %all-gather.1 = f32[128,32]{1,0:T(8,128)S(1)} all-gather(f32[32,32]{1,0:T(8,128)S(1)} %copy.208), channel_id=3, replica_groups=mesh['grp'=4,'sub'=8] {'grp'}, dimensions={0}, use_global_device_ids=true | all-gather | bytes 20480 | tf_op jit(solution)/shard_map/all_gather | solution.py:163
  184.6 5.9 %custom-call.59 = f32[2,32,32]{2,1,0:T(8,128)S(1)} custom-call(f32[2,32,32]{2,1,0:T(8,128)S(1)} %fusion.112), custom_call_target="Cholesky" | custom-call | tf_op jit(solution)/shard_map/jit(cholesky)/cholesky | solution.py:55
  190.7 4.9 %custom-call.52 = f32[2,1,32,32]{2,3,1,0:T(8,128)S(1)} custom-call(f32[2,1,32,32]{3,2,1,0:T(8,128)S(1)} %fusion.118), custom_call_target="InvertDiagBlocksLowerTriangular" | custom-call | tf_op jit(solution)/shard_map/triangular_solve | solution.py:26
  197.6 2.9 %custom-call.60 = f32[1,32,32]{2,1,0:T(8,128)S(1)} custom-call(f32[1,32,32]{2,1,0:T(8,128)S(1)} %fusion.158), custom_call_target="Cholesky" | custom-call | tf_op jit(solution)/shard_map/jit(cholesky)/cholesky | solution.py:55
  201.9 2.4 custom-call.53
  205.5 2.9 %cholesky.216 = f32[32,32]{1,0:T(8,128)S(1)} custom-call(f32[32,32]{1,0:T(8,128)S(1)} %fusion.149), custom_call_target="Cholesky" | custom-call | tf_op jit(solution)/shard_map/jit(cholesky)/cholesky | solution.py:74
  209.8 2.4 custom-call.54
  217.3 2.4 collective-permute-start.4
  220.1 4.3 %collective-permute-done.4 = bf16[1,128,160]{1,2,0:T(8,128)(2,1)S(1)} collective-permute-done((bf16[1,128,160]{1,2,0:T(8,128)(2,1)S(1)}, bf16[1,128,160]{1,2,0:T(8,128)(2,1)S(1)}, u32[]{:S(2)}, u32[]{:S(2)}) %collective-permute-start.4) | collective-permute-done | bytes 40992 | tf_op jit(solution)/shard_map/ppermute | solution.py:15
  233.4 2.4 collective-permute-start.6
  238.6 3.1 %collective-permute-done.6 = bf16[1,128,160]{2,1,0:T(8,128)(2,1)S(1)} collective-permute-done((bf16[1,128,160]{2,1,0:T(8,128)(2,1)S(1)}, bf16[1,128,160]{2,1,0:T(8,128)(2,1)S(1)}, u32[]{:S(2)}, u32[]{:S(2)}) %collective-permute-start.6) | collective-permute-done | bytes 40992 | tf_op jit(solution)/shard_map/ppermute | solution.py:15
  242.8 44.1 %all-reduce.16 = (f32[160]{0:T(256)S(1)}, f32[160]{0:T(256)S(1)}) all-reduce(f32[160]{0:T(256)S(1)} %get-tuple-element.30, f32[160]{0:T(256)S(1)} %get-tuple-element.29), channel_id=1, replica_groups=mesh['grp'=4,'sub'=8] {'grp','sub'}, use_global_device_ids=true, to_apply=%region_11.15 | all-reduce | flops 320 | bytes 2560 | tf_op jit(solution)/shard_map/psum | solution.py:191
  286.9 2.3 multiply_subtract_fusion
  (282 shorter events, 58.2 us)
Async XLA Ops:
  0.6 213.9 %copy-start = (bf16[1,1024,1024]{2,1,0:T(8,128)(2,1)S(1)}, bf16[1,1024,1024]{2,1,0:T(8,128)(2,1)}, u32[]{:S(2)}) copy-start(bf16[1,1024,1024]{2,1,0:T(8,128)(2,1)} %param.27) | copy-start | bytes 6291460
  0.6 9.5 %copy-start.43 = (s32[1,6,3]{1,0,2:T(1,128)S(1)}, s32[1,6,3]{1,0,2:T(1,128)}, u32[]{:S(2)}) copy-start(s32[1,6,3]{1,0,2:T(1,128)} %param.23) | copy-start | bytes 220
  0.7 9.7 %copy-start.34 = (f32[1,32,32]{2,1,0:T(8,128)S(1)}, f32[1,32,32]{2,1,0:T(8,128)}, u32[]{:S(2)}) copy-start(f32[1,32,32]{2,1,0:T(8,128)} %param.30) | copy-start | bytes 12292
  0.7 24.5 %copy-start.35 = (f32[1,32,32]{2,1,0:T(8,128)S(1)}, f32[1,32,32]{2,1,0:T(8,128)}, u32[]{:S(2)}) copy-start(f32[1,32,32]{2,1,0:T(8,128)} %param.29) | copy-start | bytes 12292
  2.8 7.3 %copy-start.38 = (s32[128]{0:T(128)}, s32[128]{0:T(128)S(1)}, u32[]{:S(2)}) copy-start(s32[128]{0:T(128)S(1)} %get-tuple-element.52) | copy-start | bytes 1540
  2.8 22.4 %copy-start.40 = (s32[128]{0:T(128)}, s32[128]{0:T(128)S(1)}, u32[]{:S(2)}) copy-start(s32[128]{0:T(128)S(1)} %get-tuple-element.51) | copy-start | bytes 1540
  2.8 22.4 %copy-start.36 = (s32[1024]{0:T(1024)}, s32[1024]{0:T(1024)S(1)}, u32[]{:S(2)}) copy-start(s32[1024]{0:T(1024)S(1)} %get-tuple-element.59) | copy-start | bytes 12292
  2.8 22.4 %copy-start.37 = (s32[1024]{0:T(1024)}, s32[1024]{0:T(1024)S(1)}, u32[]{:S(2)}) copy-start(s32[1024]{0:T(1024)S(1)} %get-tuple-element.58) | copy-start | bytes 12292
  4.3 52.1 %collective-permute-start.1 = (bf16[1,128,160]{2,1,0:T(8,128)(2,1)}, bf16[1,128,160]{2,1,0:T(8,128)(2,1)}, u32[]{:S(2)}, u32[]{:S(2)}) collective-permute-start(bf16[1,128,160]{2,1,0:T(8,128)(2,1)} %bitcast.13), channel_id=1, source_target_pairs={{1,0},{2,1},{3,2},{4,3},{5,4},{6,5},{7,6},{8,7},{9,8},{10,9},{11,1... | collective-permute-start | bytes 122888 | tf_op jit(solution)/shard_map/ppermute | solution.py:17
  7.7 49.8 %collective-permute-start = (bf16[1,128,160]{2,1,0:T(8,128)(2,1)}, bf16[1,128,160]{2,1,0:T(8,128)(2,1)}, u32[]{:S(2)}, u32[]{:S(2)}) collective-permute-start(bf16[1,128,160]{2,1,0:T(8,128)(2,1)} %bitcast.9), channel_id=1, source_target_pairs={{0,1},{1,2},{2,3},{3,4},{4,5},{5,6},{6,7},{7,8},{8,9},{9,10},{10,1... | collective-permute-start | bytes 122888 | tf_op jit(solution)/shard_map/ppermute | solution.py:15
  10.1 43.6 %copy-start.24 = (pred[32,32]{1,0:T(8,128)(4,1)}, pred[32,32]{1,0:T(8,128)(4,1)S(1)}, u32[]{:S(2)}) copy-start(pred[32,32]{1,0:T(8,128)(4,1)S(1)} %iota_compare_fusion.3) | copy-start | bytes 3076
  10.2 45.5 %copy-start.22 = (pred[32,32]{1,0:T(8,128)(4,1)}, pred[32,32]{1,0:T(8,128)(4,1)S(1)}, u32[]{:S(2)}) copy-start(pred[32,32]{1,0:T(8,128)(4,1)S(1)} %iota_compare_fusion.7) | copy-start | bytes 3076
  10.4 43.3 %copy-start.30 = (s32[1024]{0:T(1024)}, s32[1024]{0:T(1024)S(1)}, u32[]{:S(2)}) copy-start(s32[1024]{0:T(1024)S(1)} %pad_clamp_fusion.2) | copy-start | bytes 12292
  39.2 12.7 %copy-start.11 = (f32[8,32,32]{2,1,0:T(8,128)}, f32[8,32,32]{2,1,0:T(8,128)S(1)}, u32[]{:S(2)}) copy-start(f32[8,32,32]{2,1,0:T(8,128)S(1)} %all_gather.30) | copy-start | bytes 98308
  56.4 46.9 %copy-start.13 = (f32[1,32,32]{2,1,0:T(8,128)}, f32[1,32,32]{2,1,0:T(8,128)S(1)}, u32[]{:S(2)}) copy-start(f32[1,32,32]{2,1,0:T(8,128)S(1)} %get-tuple-element.38) | copy-start | bytes 12292
  59.5 20.4 %slice-start.1 = ((f32[8,32,32]{2,1,0:T(8,128)}), f32[1,32,32]{2,1,0:T(8,128)S(1)}, s32[]{:S(2)}) async-start(f32[8,32,32]{2,1,0:T(8,128)} %copy-done.11), calls=%async_computation.1 | async-start | bytes 32768 | tf_op jit(solution)/shard_map/slice | solution.py:161
  59.6 30.7 %copy-start.20 = (bf16[1,1024,32]{1,2,0:T(8,128)(2,1)S(1)}, bf16[1,1024,32]{1,2,0:T(8,128)(2,1)}, u32[]{:S(2)}) copy-start(bf16[1,1024,32]{1,2,0:T(8,128)(2,1)} %param.28) | copy-start | bytes 196612
  61.8 27.9 %collective-permute-start.3 = (bf16[1,128,160]{1,2,0:T(8,128)(2,1)S(1)}, bf16[1,128,160]{1,2,0:T(8,128)(2,1)S(1)}, u32[]{:S(2)}, u32[]{:S(2)}) collective-permute-start(bf16[1,128,160]{1,2,0:T(8,128)(2,1)S(1)} %bitcast.412), channel_id=1, source_target_pairs={{1,0},{2,1},{3,2},{4,3},{5,4},{6,5},{7,6},{8,7},{9,8},{10,9},{11,1... | collective-permute-start | bytes 122888 | tf_op jit(solution)/shard_map/ppermute | solution.py:17
  65.9 23.7 %collective-permute-start.2 = (bf16[1,128,160]{1,2,0:T(8,128)(2,1)S(1)}, bf16[1,128,160]{1,2,0:T(8,128)(2,1)S(1)}, u32[]{:S(2)}, u32[]{:S(2)}) collective-permute-start(bf16[1,128,160]{1,2,0:T(8,128)(2,1)S(1)} %bitcast.413), channel_id=1, source_target_pairs={{0,1},{1,2},{2,3},{3,4},{4,5},{5,6},{6,7},{7,8},{8,9},{9,10},{10,1... | collective-permute-start | bytes 122888 | tf_op jit(solution)/shard_map/ppermute | solution.py:15
  90.3 13.0 %copy-start.18 = (f32[4,1,32,32]{2,3,1,0:T(8,128)S(1)}, f32[4,1,32,32]{2,3,1,0:T(8,128)}, u32[]{:S(2)}) copy-start(f32[4,1,32,32]{2,3,1,0:T(8,128)} %custom-call.48) | copy-start | bytes 49156
  90.3 13.1 %copy-start.19 = (f32[4,32,32]{2,1,0:T(8,128)S(1)}, f32[4,32,32]{2,1,0:T(8,128)}, u32[]{:S(2)}) copy-start(f32[4,32,32]{2,1,0:T(8,128)} %copy.187) | copy-start | bytes 49156
  104.5 7.3 %copy-start.25 = (pred[32,32]{1,0:T(8,128)(4,1)S(1)}, pred[32,32]{1,0:T(8,128)(4,1)}, u32[]{:S(2)}) copy-start(pred[32,32]{1,0:T(8,128)(4,1)} %copy-done.24) | copy-start | bytes 3076
  104.5 7.5 %copy-start.23 = (pred[32,32]{1,0:T(8,128)(4,1)S(1)}, pred[32,32]{1,0:T(8,128)(4,1)}, u32[]{:S(2)}) copy-start(pred[32,32]{1,0:T(8,128)(4,1)} %copy-done.22) | copy-start | bytes 3076
  135.2 33.1 %copy-start.44 = (pred[4]{0:T(512)(128)(4,1)S(1)}, pred[4]{0:T(512)(128)(4,1)}, u32[]{:S(2)}) copy-start(pred[4]{0:T(512)(128)(4,1)} %constant.263.clone.1) | copy-start | bytes 16
  152.4 32.1 %copy-start.17 = (f32[4,32,32]{1,2,0:T(8,128)S(1)}, f32[4,32,32]{1,2,0:T(8,128)}, u32[]{:S(2)}) copy-start(f32[4,32,32]{1,2,0:T(8,128)} %copy.210) | copy-start | bytes 49156
  215.4 4.7 %collective-permute-start.5 = (bf16[1,128,160]{1,2,0:T(8,128)(2,1)S(1)}, bf16[1,128,160]{1,2,0:T(8,128)(2,1)S(1)}, u32[]{:S(2)}, u32[]{:S(2)}) collective-permute-start(bf16[1,128,160]{1,2,0:T(8,128)(2,1)S(1)} %get-tuple-element.34), channel_id=1, source_target_pairs={{1,0},{2,1},{3,2},{4,3},{5,4},{6,5},{7,6},{8,7},{9,8},{10,9},{11,1... | collective-permute-start | bytes 122888 | tf_op jit(solution)/shard_map/ppermute | solution.py:17
  217.3 7.1 %collective-permute-start.4 = (bf16[1,128,160]{1,2,0:T(8,128)(2,1)S(1)}, bf16[1,128,160]{1,2,0:T(8,128)(2,1)S(1)}, u32[]{:S(2)}, u32[]{:S(2)}) collective-permute-start(bf16[1,128,160]{1,2,0:T(8,128)(2,1)S(1)} %get-tuple-element.33), channel_id=1, source_target_pairs={{0,1},{1,2},{2,3},{3,4},{4,5},{5,6},{6,7},{7,8},{8,9},{9,10},{10,1... | collective-permute-start | bytes 122888 | tf_op jit(solution)/shard_map/ppermute | solution.py:15
  228.9 7.1 %copy-start.31 = (s32[1024]{0:T(1024)S(1)}, s32[1024]{0:T(1024)}, u32[]{:S(2)}) copy-start(s32[1024]{0:T(1024)} %copy-done.30) | copy-start | bytes 12292
  231.4 6.9 %collective-permute-start.7 = (bf16[1,128,160]{2,1,0:T(8,128)(2,1)}, bf16[1,128,160]{2,1,0:T(8,128)(2,1)S(1)}, u32[]{:S(2)}, u32[]{:S(2)}) collective-permute-start(bf16[1,128,160]{2,1,0:T(8,128)(2,1)} %bitcast.124), channel_id=1, source_target_pairs={{1,0},{2,1},{3,2},{4,3},{5,4},{6,5},{7,6},{8,7},{9,8},{10,9},{11,1... | collective-permute-start | bytes 122888 | tf_op jit(solution)/shard_map/ppermute | solution.py:17
  233.4 8.3 %collective-permute-start.6 = (bf16[1,128,160]{2,1,0:T(8,128)(2,1)S(1)}, bf16[1,128,160]{2,1,0:T(8,128)(2,1)S(1)}, u32[]{:S(2)}, u32[]{:S(2)}) collective-permute-start(bf16[1,128,160]{2,1,0:T(8,128)(2,1)S(1)} %bitcast.407), channel_id=1, source_target_pairs={{0,1},{1,2},{2,3},{3,4},{4,5},{5,6},{6,7},{7,8},{8,9},{9,10},{10,1... | collective-permute-start | bytes 122888 | tf_op jit(solution)/shard_map/ppermute | solution.py:15
  236.7 4.9 %copy-start.3 = (f32[768,160]{0,1:T(8,128)S(1)}, f32[768,160]{0,1:T(8,128)}, u32[]{:S(2)}) copy-start(f32[768,160]{0,1:T(8,128)} %get-tuple-element.54) | copy-start | bytes 1474564
  241.7 45.2 %copy-start.2 = (f32[768,160]{0,1:T(8,128)S(1)}, f32[768,160]{0,1:T(8,128)}, u32[]{:S(2)}) copy-start(f32[768,160]{0,1:T(8,128)} %param.20) | copy-start | bytes 1474564
  (23 other events, 56.1 us)
where the time goes:
time: 290 us; the launch traced here: 289 us
  blocking collectives  142 us (49%)
  other arithmetic  79.4 us (27%)
  matrix products  21.8 us (8%)
  starting transfers between devices  18.9 us (7%)
  local copies, waits for them, and re-layouts  17.4 us (6%)
  waiting for transfers between devices  7.38 us (3%)
    psum x1, blocking collectives, shards(): inner = lax.psum(jnp.sum(residual_start * owned, axis=0), ('grp', 'sub'))  44.1 us
    another operation x15, other arithmetic, chol_solve(): lax.linalg.triangular_solve(factor, halfway, left_side=True, lower=True,...  34 us
    another operation x15, other arithmetic, solve_chain(): factor = jnp.linalg.cholesky(diag_odd)  31.6 us
    all_gather x1, blocking collectives, shards(): blocks_up = lax.all_gather(coarse_up, 'sub', axis=0, tiled=True)  14.8 us
    all_gather x1, blocking collectives, shards(): blocks_diag = lax.all_gather(coarse_diag, 'sub', axis=0, tiled=True)  14 us
    all_gather x1, blocking collectives, shards(): columns = lax.all_gather(coarse_in[None], 'sub', axis=0, tiled=True)  12.7 us
    ppermute x4, starting transfers between devices, with_halo(): lax.ppermute(head, axis, [((i + 1) % count, i) for i in range(ends)])  9.75 us
    ppermute x4, starting transfers between devices, with_halo(): lax.ppermute(tail, axis, [(i, (i + 1) % count) for i in range(ends)])  9.13 us
  transfers between devices with their start and end apart: 8, of which 2 were waited for; matrix products, arithmetic and copies ran while one was open for 12% of the time, Pallas kernels for 0%

commit v1 on v0

--- a/solution.py
+++ b/solution.py
@@ -133,8 +133,11 @@
     extended = jnp.concatenate([from_left, rounded, from_right], axis=0)
     local_part = jnp.dot(local_inverse[0], extended, preferred_element_type=f32)
     coarse_in = jnp.dot(coarse_basis[0].T, extended, preferred_element_type=f32)
-    blocks_diag = lax.all_gather(coarse_diag, "sub", axis=0, tiled=True)
-    blocks_up = lax.all_gather(coarse_up, "sub", axis=0, tiled=True)
+    blocks_diag, blocks_up = jnp.split(
+        lax.all_gather(jnp.concatenate([coarse_diag, coarse_up], 1), "sub", axis=0, tiled=True),
+        [coarse_diag.shape[1]],
+        1,
+    )
     group = lax.axis_index("grp")
     groups = lax.axis_size("grp")
     member = lax.axis_index("sub")

time: 290 us -> 277 us (0.955)
  blocking collectives: 142 us -> 128 us
    all_gather x2 -> x1, blocking collectives: 28.8 us -> 14.8 us  [shards(): lax.all_gather(jnp.concatenate([coarse_diag, coarse_up], 1), 'sub', axis=...]
  transfers between devices with their start and end apart: 8 -> 8, of which waited for: 2 -> 2; matrix products, arithmetic and copies ran while one was open for 12% -> 13% of each run, Pallas kernels for 0% -> 0%
where the time goes in v1:
time: 277 us; the launch traced here: 276 us
  blocking collectives  128 us (46%)
  other arithmetic  78.4 us (28%)
  matrix products  23.9 us (9%)
  starting transfers between devices  19 us (7%)
  local copies, waits for them, and re-layouts  18.1 us (7%)
  waiting for transfers between devices  7.18 us (3%)
    psum x1, blocking collectives, shards(): inner = lax.psum(jnp.sum(residual_start * owned, axis=0), ('grp', 'sub'))  44 us
    another operation x15, other arithmetic, chol_solve(): lax.linalg.triangular_solve(factor, halfway, left_side=True, lower=True,...  33.4 us
    another operation x15, other arithmetic, solve_chain(): factor = jnp.linalg.cholesky(diag_odd)  31.1 us
    all_gather x1, blocking collectives, shards(): lax.all_gather(jnp.concatenate([coarse_diag, coarse_up], 1), 'sub', axis=...  14.8 us
    all_gather x1, blocking collectives, shards(): columns = lax.all_gather(coarse_in[None], 'sub', axis=0, tiled=True)  12.6 us
    ppermute x4, starting transfers between devices, with_halo(): lax.ppermute(head, axis, [((i + 1) % count, i) for i in range(ends)])  9.74 us
    ppermute x4, starting transfers between devices, with_halo(): lax.ppermute(tail, axis, [(i, (i + 1) % count) for i in range(ends)])  9.26 us
    all_gather x1, blocking collectives, shards(): sep_diag = lax.all_gather(blocks_diag[0][None], 'grp', axis=0, tiled=True)  9.15 us
  transfers between devices with their start and end apart: 8, of which 2 were waited for; matrix products, arithmetic and copies ran while one was open for 13% of the time, Pallas kernels for 0%

profile of v1, /device:TPU:14, one launch (start us, length us, event | category | flops | bytes accessed | tf_op | source)
XLA Modules:
  0.0 276.5 jit_solution(5744152598723178158)
XLA Ops:
  7.7 2.4 collective-permute-start
  10.4 14.8 %all_gather.27 = f32[8,64,32]{1,2,0:T(8,128)S(1)} all-gather(f32[1,64,32]{1,2,0:T(8,128)S(1)} %pad_maximum_fusion.14), channel_id=1, replica_groups=mesh['grp'=4,'sub'=8] {'sub'}, dimensions={0}, use_global_device_ids=true | all-gather | bytes 73728 | tf_op jit(solution)/shard_map/all_gather | solution.py:137
  26.4 11.7 %custom-call.47 = f32[4,32,32]{2,1,0:T(8,128)S(1)} custom-call(f32[4,32,32]{2,1,0:T(8,128)S(1)} %copy.192), custom_call_target="Cholesky" | custom-call | tf_op jit(solution)/shard_map/jit(cholesky)/cholesky | solution.py:55
  40.0 2.6 convolution_bitcast_fusion.1
  49.1 4.0 %collective-permute-start.3 = (bf16[1,128,160]{1,2,0:T(8,128)(2,1)S(1)}, bf16[1,128,160]{1,2,0:T(8,128)(2,1)S(1)}, u32[]{:S(2)}, u32[]{:S(2)}) collective-permute-start(bf16[1,128,160]{1,2,0:T(8,128)(2,1)S(1)} %bitcast.403), channel_id=1, source_target_pairs={{1,0},{2,1},{3,2},{4,3},{5,4},{6,5},{7,6},{8,7},{9,8},{10,9},{11,1... | collective-permute-start | bytes 122888 | tf_op jit(solution)/shard_map/ppermute | solution.py:17
  56.0 10.5 %custom-call.48 = f32[4,1,32,32]{2,3,1,0:T(8,128)S(1)} custom-call(f32[4,1,32,32]{3,2,1,0:T(8,128)} %select_bitcast_fusion), custom_call_target="InvertDiagBlocksLowerTriangular" | custom-call | tf_op jit(solution)/shard_map/triangular_solve | solution.py:26
  66.7 9.2 %all_gather.28 = f32[4,32,32]{2,1,0:T(8,128)S(1)} all-gather(f32[1,32,32]{2,1,0:T(8,128)S(1)} %copy.189), channel_id=1, replica_groups=mesh['grp'=4,'sub'=8] {'grp'}, dimensions={0}, use_global_device_ids=true | all-gather | bytes 20480 | tf_op jit(solution)/shard_map/all_gather | solution.py:164
  77.4 12.6 %all-gather = f32[256,160]{1,0:T(8,128)S(1)} all-gather(f32[32,160]{1,0:T(8,128)S(1)} %convolution_bitcast_fusion.10), channel_id=2, replica_groups=mesh['grp'=4,'sub'=8] {'sub'}, dimensions={0}, use_global_device_ids=true | all-gather | bytes 184320 | tf_op jit(solution)/shard_map/all_gather | solution.py:148
  93.6 5.9 %custom-call.57 = f32[2,32,32]{2,1,0:T(8,128)S(1)} custom-call(f32[2,32,32]{2,1,0:T(8,128)S(1)} %fusion.118), custom_call_target="Cholesky" | custom-call | tf_op jit(solution)/shard_map/jit(cholesky)/cholesky | solution.py:55
  99.7 4.9 %custom-call.49 = f32[2,1,32,32]{2,3,1,0:T(8,128)S(1)} custom-call(f32[2,1,32,32]{3,2,1,0:T(8,128)S(1)} %fusion.120), custom_call_target="InvertDiagBlocksLowerTriangular" | custom-call | tf_op jit(solution)/shard_map/triangular_solve | solution.py:26
  106.7 2.9 %custom-call.58 = f32[1,32,32]{2,1,0:T(8,128)S(1)} custom-call(f32[1,32,32]{2,1,0:T(8,128)S(1)} %fusion.169), custom_call_target="Cholesky" | custom-call | tf_op jit(solution)/shard_map/jit(cholesky)/cholesky | solution.py:55
  110.9 2.4 custom-call.50
  114.5 2.9 %cholesky.184 = f32[32,32]{1,0:T(8,128)S(1)} custom-call(f32[32,32]{1,0:T(8,128)S(1)} %fusion.150), custom_call_target="Cholesky" | custom-call | tf_op jit(solution)/shard_map/jit(cholesky)/cholesky | solution.py:74
  118.7 2.4 custom-call.51
  124.2 7.0 %all-gather.6 = f32[128,160]{1,0:T(8,128)S(1)} all-gather(f32[32,160]{1,0:T(8,128)S(1)} %slice-done), channel_id=8, replica_groups=mesh['grp'=4,'sub'=8] {'grp'}, dimensions={0}, use_global_device_ids=true | all-gather | bytes 102400 | tf_op jit(solution)/shard_map/all_gather | solution.py:165
  131.2 8.9 %all-gather.4 = f32[128,160]{1,0:T(8,128)S(1)} all-gather(f32[32,160]{1,0:T(8,128)S(1)} %fusion.102), channel_id=6, replica_groups=mesh['grp'=4,'sub'=8] {'grp'}, dimensions={0}, use_global_device_ids=true | all-gather | bytes 102400 | tf_op jit(solution)/shard_map/all_gather | solution.py:169
  140.2 7.3 %all-gather.5 = f32[128,160]{1,0:T(8,128)S(1)} all-gather(f32[32,160]{1,0:T(8,128)S(1)} %fusion.101), channel_id=7, replica_groups=mesh['grp'=4,'sub'=8] {'grp'}, dimensions={0}, use_global_device_ids=true | all-gather | bytes 102400 | tf_op jit(solution)/shard_map/all_gather | solution.py:170
  147.5 8.7 %all-gather.3 = f32[128,32]{1,0:T(8,128)S(1)} all-gather(f32[32,32]{1,0:T(8,128)S(1)} %fusion.146), channel_id=5, replica_groups=mesh['grp'=4,'sub'=8] {'grp'}, dimensions={0}, use_global_device_ids=true | all-gather | bytes 20480 | tf_op jit(solution)/shard_map/all_gather | solution.py:168
  156.4 6.8 %all-gather.2 = f32[128,32]{1,0:T(8,128)S(1)} all-gather(f32[32,32]{1,0:T(8,128)S(1)} %fusion.147), channel_id=4, replica_groups=mesh['grp'=4,'sub'=8] {'grp'}, dimensions={0}, use_global_device_ids=true | all-gather | bytes 20480 | tf_op jit(solution)/shard_map/all_gather | solution.py:167
  163.3 8.7 %all-gather.1 = f32[128,32]{1,0:T(8,128)S(1)} all-gather(f32[32,32]{1,0:T(8,128)S(1)} %fusion.148), channel_id=3, replica_groups=mesh['grp'=4,'sub'=8] {'grp'}, dimensions={0}, use_global_device_ids=true | all-gather | bytes 20480 | tf_op jit(solution)/shard_map/all_gather | solution.py:166
  172.2 5.9 %custom-call.59 = f32[2,32,32]{2,1,0:T(8,128)S(1)} custom-call(f32[2,32,32]{2,1,0:T(8,128)S(1)} %fusion.113), custom_call_target="Cholesky" | custom-call | tf_op jit(solution)/shard_map/jit(cholesky)/cholesky | solution.py:55
  178.3 4.9 %custom-call.52 = f32[2,1,32,32]{2,3,1,0:T(8,128)S(1)} custom-call(f32[2,1,32,32]{3,2,1,0:T(8,128)S(1)} %fusion.119), custom_call_target="InvertDiagBlocksLowerTriangular" | custom-call | tf_op jit(solution)/shard_map/triangular_solve | solution.py:26
  185.3 2.9 %custom-call.60 = f32[1,32,32]{2,1,0:T(8,128)S(1)} custom-call(f32[1,32,32]{2,1,0:T(8,128)S(1)} %fusion.158), custom_call_target="Cholesky" | custom-call | tf_op jit(solution)/shard_map/jit(cholesky)/cholesky | solution.py:55
  189.5 2.4 custom-call.53
  193.2 2.9 %cholesky.216 = f32[32,32]{1,0:T(8,128)S(1)} custom-call(f32[32,32]{1,0:T(8,128)S(1)} %fusion.149), custom_call_target="Cholesky" | custom-call | tf_op jit(solution)/shard_map/jit(cholesky)/cholesky | solution.py:74
  197.4 2.4 custom-call.54
  204.9 2.4 collective-permute-start.4
  207.7 4.1 %collective-permute-done.4 = bf16[1,128,160]{1,2,0:T(8,128)(2,1)S(1)} collective-permute-done((bf16[1,128,160]{1,2,0:T(8,128)(2,1)S(1)}, bf16[1,128,160]{1,2,0:T(8,128)(2,1)S(1)}, u32[]{:S(2)}, u32[]{:S(2)}) %collective-permute-start.4) | collective-permute-done | bytes 40992 | tf_op jit(solution)/shard_map/ppermute | solution.py:15
  220.8 2.4 collective-permute-start.6
  226.0 3.1 %collective-permute-done.6 = bf16[1,128,160]{2,1,0:T(8,128)(2,1)S(1)} collective-permute-done((bf16[1,128,160]{2,1,0:T(8,128)(2,1)S(1)}, bf16[1,128,160]{2,1,0:T(8,128)(2,1)S(1)}, u32[]{:S(2)}, u32[]{:S(2)}) %collective-permute-start.6) | collective-permute-done | bytes 40992 | tf_op jit(solution)/shard_map/ppermute | solution.py:15
  230.2 44.0 %all-reduce.16 = (f32[160]{0:T(256)S(1)}, f32[160]{0:T(256)S(1)}) all-reduce(f32[160]{0:T(256)S(1)} %get-tuple-element.30, f32[160]{0:T(256)S(1)} %get-tuple-element.29), channel_id=1, replica_groups=mesh['grp'=4,'sub'=8] {'grp','sub'}, use_global_device_ids=true, to_apply=%region_11.15 | all-reduce | flops 320 | bytes 2560 | tf_op jit(solution)/shard_map/psum | solution.py:194
  274.2 2.3 multiply_subtract_fusion
  (262 shorter events, 58.1 us)
Async XLA Ops:
  0.6 201.5 %copy-start = (bf16[1,1024,1024]{2,1,0:T(8,128)(2,1)S(1)}, bf16[1,1024,1024]{2,1,0:T(8,128)(2,1)}, u32[]{:S(2)}) copy-start(bf16[1,1024,1024]{2,1,0:T(8,128)(2,1)} %param.27) | copy-start | bytes 6291460
  0.6 9.5 %copy-start.25 = (f32[1,32,32]{2,1,0:T(8,128)S(1)}, f32[1,32,32]{2,1,0:T(8,128)}, u32[]{:S(2)}) copy-start(f32[1,32,32]{2,1,0:T(8,128)} %param.30) | copy-start | bytes 12292
  0.7 9.6 %copy-start.26 = (f32[1,32,32]{2,1,0:T(8,128)S(1)}, f32[1,32,32]{2,1,0:T(8,128)}, u32[]{:S(2)}) copy-start(f32[1,32,32]{2,1,0:T(8,128)} %param.29) | copy-start | bytes 12292
  0.7 25.2 %copy-start.33 = (s32[1,6,3]{1,0,2:T(1,128)S(1)}, s32[1,6,3]{1,0,2:T(1,128)}, u32[]{:S(2)}) copy-start(s32[1,6,3]{1,0,2:T(1,128)} %param.23) | copy-start | bytes 220
  2.8 7.3 %copy-start.29 = (s32[128]{0:T(128)}, s32[128]{0:T(128)S(1)}, u32[]{:S(2)}) copy-start(s32[128]{0:T(128)S(1)} %get-tuple-element.53) | copy-start | bytes 1540
  2.8 7.3 %copy-start.31 = (s32[128]{0:T(128)}, s32[128]{0:T(128)S(1)}, u32[]{:S(2)}) copy-start(s32[128]{0:T(128)S(1)} %get-tuple-element.52) | copy-start | bytes 1540
  2.8 7.3 %copy-start.27 = (s32[1024]{0:T(1024)}, s32[1024]{0:T(1024)S(1)}, u32[]{:S(2)}) copy-start(s32[1024]{0:T(1024)S(1)} %get-tuple-element.60) | copy-start | bytes 12292
  2.8 7.3 %copy-start.28 = (s32[1024]{0:T(1024)}, s32[1024]{0:T(1024)S(1)}, u32[]{:S(2)}) copy-start(s32[1024]{0:T(1024)S(1)} %get-tuple-element.59) | copy-start | bytes 12292
  4.3 39.2 %collective-permute-start.1 = (bf16[1,128,160]{2,1,0:T(8,128)(2,1)}, bf16[1,128,160]{2,1,0:T(8,128)(2,1)}, u32[]{:S(2)}, u32[]{:S(2)}) collective-permute-start(bf16[1,128,160]{2,1,0:T(8,128)(2,1)} %bitcast.13), channel_id=1, source_target_pairs={{1,0},{2,1},{3,2},{4,3},{5,4},{6,5},{7,6},{8,7},{9,8},{10,9},{11,1... | collective-permute-start | bytes 122888 | tf_op jit(solution)/shard_map/ppermute | solution.py:17
  7.7 36.9 %collective-permute-start = (bf16[1,128,160]{2,1,0:T(8,128)(2,1)}, bf16[1,128,160]{2,1,0:T(8,128)(2,1)}, u32[]{:S(2)}, u32[]{:S(2)}) collective-permute-start(bf16[1,128,160]{2,1,0:T(8,128)(2,1)} %bitcast.9), channel_id=1, source_target_pairs={{0,1},{1,2},{2,3},{3,4},{4,5},{5,6},{6,7},{7,8},{8,9},{9,10},{10,1... | collective-permute-start | bytes 122888 | tf_op jit(solution)/shard_map/ppermute | solution.py:15
  26.2 12.1 %copy-start.7 = (f32[8,32,32]{1,2,0:T(8,128)}, f32[8,32,32]{1,2,0:T(8,128)S(1)}, u32[]{:S(2)}) copy-start(f32[8,32,32]{1,2,0:T(8,128)S(1)} %pad_maximum_fusion.4) | copy-start | bytes 98308
  40.0 3.5 %copy-start.11 = (bf16[768,128]{1,0:T(8,128)(2,1)S(1)}, bf16[768,128]{1,0:T(8,128)(2,1)}, u32[]{:S(2)}) copy-start(bf16[768,128]{1,0:T(8,128)(2,1)} %param.25) | copy-start | bytes 589828
  42.6 2.0 copy-start.24
  46.9 19.7 %copy-start.19 = (f32[1,32,32]{1,2,0:T(8,128)S(1)}, f32[1,32,32]{1,2,0:T(8,128)}, u32[]{:S(2)}) copy-start(f32[1,32,32]{1,2,0:T(8,128)} %get-tuple-element.37) | copy-start | bytes 12292
  46.9 30.3 %copy-start.16 = (bf16[1,1024,32]{1,2,0:T(8,128)(2,1)S(1)}, bf16[1,1024,32]{1,2,0:T(8,128)(2,1)}, u32[]{:S(2)}) copy-start(bf16[1,1024,32]{1,2,0:T(8,128)(2,1)} %param.28) | copy-start | bytes 196612
  49.1 27.4 %collective-permute-start.3 = (bf16[1,128,160]{1,2,0:T(8,128)(2,1)S(1)}, bf16[1,128,160]{1,2,0:T(8,128)(2,1)S(1)}, u32[]{:S(2)}, u32[]{:S(2)}) collective-permute-start(bf16[1,128,160]{1,2,0:T(8,128)(2,1)S(1)} %bitcast.403), channel_id=1, source_target_pairs={{1,0},{2,1},{3,2},{4,3},{5,4},{6,5},{7,6},{8,7},{9,8},{10,9},{11,1... | collective-permute-start | bytes 122888 | tf_op jit(solution)/shard_map/ppermute | solution.py:17
  53.3 36.7 %copy-start.18 = (f32[1,32,32]{2,1,0:T(8,128)S(1)}, f32[1,32,32]{2,1,0:T(8,128)}, u32[]{:S(2)}) copy-start(f32[1,32,32]{2,1,0:T(8,128)} %get-tuple-element.38) | copy-start | bytes 12292
  53.3 23.3 %collective-permute-start.2 = (bf16[1,128,160]{1,2,0:T(8,128)(2,1)S(1)}, bf16[1,128,160]{1,2,0:T(8,128)(2,1)S(1)}, u32[]{:S(2)}, u32[]{:S(2)}) collective-permute-start(bf16[1,128,160]{1,2,0:T(8,128)(2,1)S(1)} %bitcast.404), channel_id=1, source_target_pairs={{0,1},{1,2},{2,3},{3,4},{4,5},{5,6},{6,7},{7,8},{8,9},{9,10},{10,1... | collective-permute-start | bytes 122888 | tf_op jit(solution)/shard_map/ppermute | solution.py:15
  66.6 23.5 %copy-start.14 = (f32[4,1,32,32]{2,3,1,0:T(8,128)}, f32[4,1,32,32]{2,3,1,0:T(8,128)S(1)}, u32[]{:S(2)}) copy-start(f32[4,1,32,32]{2,3,1,0:T(8,128)S(1)} %custom-call.48) | copy-start | bytes 49156
  77.2 12.9 %copy-start.15 = (f32[4,32,32]{2,1,0:T(8,128)S(1)}, f32[4,32,32]{2,1,0:T(8,128)}, u32[]{:S(2)}) copy-start(f32[4,32,32]{2,1,0:T(8,128)} %copy.194) | copy-start | bytes 49156
  90.6 2.6 copy-start.8
  122.9 33.4 %copy-start.34 = (pred[4]{0:T(512)(128)(4,1)S(1)}, pred[4]{0:T(512)(128)(4,1)}, u32[]{:S(2)}) copy-start(pred[4]{0:T(512)(128)(4,1)} %constant.263.clone.1) | copy-start | bytes 16
  140.2 31.9 %copy-start.13 = (f32[4,32,32]{1,2,0:T(8,128)S(1)}, f32[4,32,32]{1,2,0:T(8,128)}, u32[]{:S(2)}) copy-start(f32[4,32,32]{1,2,0:T(8,128)} %copy.216) | copy-start | bytes 49156
  203.0 4.7 %collective-permute-start.5 = (bf16[1,128,160]{1,2,0:T(8,128)(2,1)S(1)}, bf16[1,128,160]{1,2,0:T(8,128)(2,1)S(1)}, u32[]{:S(2)}, u32[]{:S(2)}) collective-permute-start(bf16[1,128,160]{1,2,0:T(8,128)(2,1)S(1)} %get-tuple-element.34), channel_id=1, source_target_pairs={{1,0},{2,1},{3,2},{4,3},{5,4},{6,5},{7,6},{8,7},{9,8},{10,9},{11,1... | collective-permute-start | bytes 122888 | tf_op jit(solution)/shard_map/ppermute | solution.py:17
  204.9 6.8 %collective-permute-start.4 = (bf16[1,128,160]{1,2,0:T(8,128)(2,1)S(1)}, bf16[1,128,160]{1,2,0:T(8,128)(2,1)S(1)}, u32[]{:S(2)}, u32[]{:S(2)}) collective-permute-start(bf16[1,128,160]{1,2,0:T(8,128)(2,1)S(1)} %get-tuple-element.33), channel_id=1, source_target_pairs={{0,1},{1,2},{2,3},{3,4},{4,5},{5,6},{6,7},{7,8},{8,9},{9,10},{10,1... | collective-permute-start | bytes 122888 | tf_op jit(solution)/shard_map/ppermute | solution.py:15
  207.4 4.6 %copy-start.32 = (s32[128]{0:T(128)S(1)}, s32[128]{0:T(128)}, u32[]{:S(2)}) copy-start(s32[128]{0:T(128)} %copy-done.31) | copy-start | bytes 1540
  218.8 6.9 %collective-permute-start.7 = (bf16[1,128,160]{2,1,0:T(8,128)(2,1)}, bf16[1,128,160]{2,1,0:T(8,128)(2,1)S(1)}, u32[]{:S(2)}, u32[]{:S(2)}) collective-permute-start(bf16[1,128,160]{2,1,0:T(8,128)(2,1)} %bitcast.121), channel_id=1, source_target_pairs={{1,0},{2,1},{3,2},{4,3},{5,4},{6,5},{7,6},{8,7},{9,8},{10,9},{11,1... | collective-permute-start | bytes 122888 | tf_op jit(solution)/shard_map/ppermute | solution.py:17
  220.8 8.3 %collective-permute-start.6 = (bf16[1,128,160]{2,1,0:T(8,128)(2,1)S(1)}, bf16[1,128,160]{2,1,0:T(8,128)(2,1)S(1)}, u32[]{:S(2)}, u32[]{:S(2)}) collective-permute-start(bf16[1,128,160]{2,1,0:T(8,128)(2,1)S(1)} %bitcast.398), channel_id=1, source_target_pairs={{0,1},{1,2},{2,3},{3,4},{4,5},{5,6},{6,7},{7,8},{8,9},{9,10},{10,1... | collective-permute-start | bytes 122888 | tf_op jit(solution)/shard_map/ppermute | solution.py:15
  224.1 4.9 %copy-start.3 = (f32[768,160]{0,1:T(8,128)S(1)}, f32[768,160]{0,1:T(8,128)}, u32[]{:S(2)}) copy-start(f32[768,160]{0,1:T(8,128)} %get-tuple-element.55) | copy-start | bytes 1474564
  224.1 4.9 %copy-start.4 = (f32[768,160]{0,1:T(8,128)S(1)}, f32[768,160]{0,1:T(8,128)}, u32[]{:S(2)}) copy-start(f32[768,160]{0,1:T(8,128)} %copy.235) | copy-start | bytes 1474564
  224.1 4.9 %copy-start.10 = (bf16[768,128]{1,0:T(8,128)(2,1)S(1)}, bf16[768,128]{1,0:T(8,128)(2,1)}, u32[]{:S(2)}) copy-start(bf16[768,128]{1,0:T(8,128)(2,1)} %param.24) | copy-start | bytes 589828
  229.0 45.1 %copy-start.2 = (f32[768,160]{0,1:T(8,128)S(1)}, f32[768,160]{0,1:T(8,128)}, u32[]{:S(2)}) copy-start(f32[768,160]{0,1:T(8,128)} %param.20) | copy-start | bytes 1474564
  (12 other events, 18.2 us)
